TPU v7x, 32 devices: a whole 2x2x4 slice. The times are simulated.
32 devices in a mesh: seq: 16 (over z, y, x), grp: 2 (over core).
Axes of the slice: x: 2, y: 2, z: 4, core: 2. Of those that a mesh axis runs over, the one named last changes fastest.
Arguments:
- key_rows: bfloat16 [32768, 4096], P('seq', 'grp')
- probe_ints: int32 [4096, 512], P('grp'), may hold values from -2 to 2
- rank_keep: int32 [1], replicated, may hold values from 128 to 511
Outputs:
- latents: float32 [32768, 512], P('seq', 'grp')
- latent_basis: float32 [512, 4096], P('seq', 'grp')
All inputs are finite; a program needn't handle non-finite values.
Results may differ from a plain program's by a relative error of at most 0.00098.
Values may be sent and summed in bfloat16 or wider, within the bound.
A program may use at most 128 MiB of HBM per device.

v0:
```python
import math
import jax
import jax.numpy as jnp
from jax import lax
from jax.sharding import PartitionSpec as P


def on_device(key_rows, probe_ints, rank_keep):
    seq_count = lax.axis_size("seq")
    tokens = key_rows.shape[0] * seq_count
    root_tokens = math.sqrt(tokens)
    probes = (probe_ints.astype(jnp.float32) * 0.015625).astype(jnp.bfloat16)
    whole_keys = lax.all_gather(key_rows, "grp", axis=1, tiled=True)
    whole_probes = lax.all_gather(probes, "grp", axis=0, tiled=True)
    sketch = jnp.dot(whole_keys, whole_probes, preferred_element_type=jnp.float32)
    contract = (((0,), (0,)), ((), ()))
    local_gram = lax.dot_general(sketch, sketch, contract, precision=lax.Precision.HIGHEST)
    gram_matrix = lax.psum(local_gram, "seq")
    lower_factor = jnp.linalg.cholesky(gram_matrix)
    identity = jnp.eye(gram_matrix.shape[0], dtype=jnp.float32)
    inverse = lax.linalg.triangular_solve(lower_factor, identity, left_side=True, lower=True)
    orthonormal = jnp.dot(sketch, inverse.T, precision=lax.Precision.HIGHEST) * root_tokens
    probe_count = orthonormal.shape[1]
    part_width = probe_count // lax.axis_size("grp")
    first_column = lax.axis_index("grp") * part_width
    columns = first_column + jnp.arange(part_width)
    own_columns = lax.dynamic_slice_in_dim(orthonormal, first_column, part_width, 1)
    latents = jnp.where(columns[None, :] < rank_keep[0], own_columns, jnp.float32(0.0))
    rounded = orthonormal.astype(jnp.bfloat16)
    rows_out = probe_count // seq_count
    summed = lax.psum_scatter(
        lax.dot_general(rounded, key_rows, contract, preferred_element_type=jnp.float32),
        "seq",
        scatter_dimension=0,
        tiled=True,
    )
    row_index = lax.axis_index("seq") * rows_out + jnp.arange(rows_out)
    latent_basis = jnp.where(
        row_index[:, None] < rank_keep[0], summed / root_tokens, jnp.float32(0.0)
    )
    return (latents, latent_basis)


def solution(mesh):
    in_specs = (P("seq", "grp"), P("grp", None), P())
    out_specs = (P("seq", "grp"), P("seq", "grp"))
    return jax.shard_map(
        on_device, mesh=mesh, in_specs=in_specs, out_specs=out_specs, check_vma=False
    )
```

profile of v0, /device:TPU:0, one launch (start us, length us, event | category | flops | bytes accessed | tf_op | source)
XLA Modules:
  0.0 463.2 jit_solution(5321967595677841850)
XLA Ops:
  7.2 4.1 multiply_convert_fusion
  11.4 0.7 all-gather.5.cloned.1.call-update
  12.1 15.7 %all-gather.3.cloned.1.call-done = bf16[4096,512]{1,0:T(8,128)(2,1)} async-done(((bf16[2048,512]{1,0:T(8,128)(2,1)}), bf16[4096,512]{1,0:T(8,128)(2,1)}) %all-gather.3.cloned.1.call-update) | async-done | bytes 4194320 | tf_op jit(solution)/shard_map/all_gather | solution.py:14
  27.8 32.8 %all-gather.5.cloned.1.call-done = bf16[2048,4096]{1,0:T(8,128)(2,1)} async-done(((bf16[2048,2048]{1,0:T(8,128)(2,1)}), bf16[2048,4096]{1,0:T(8,128)(2,1)}) %all-gather.5.cloned.1.call-update) | async-done | bytes 16777232 | tf_op jit(solution)/shard_map/all_gather | solution.py:13
  60.7 13.0 %fusion.42 = f32[512,2048]{1,0:T(8,128)S(1)} fusion(bf16[4096,512]{1,0:T(8,128)(2,1)} %all-gather.3.cloned.1.call-done, bf16[2048,4096]{1,0:T(8,128)(2,1)} %all-gather.5.cloned.1.call-done), kind=kOutput, calls=%fused_computation.84 | convolution fusion | flops 8589934592 | bytes 25165824 | tf_op jit(solution)/shard_map/dot_general | solution.py:15
  73.7 1.9 copy-done
  75.7 7.7 %fusion.43 = f32[512,512]{0,1:T(8,128)} fusion(f32[512,2048]{1,0:T(8,128)S(1)} %fusion.42), kind=kOutput, calls=%fused_computation.85 | convolution fusion | flops 6442450944 | bytes 5242880 | tf_op jit(solution)/shard_map/dot_general | solution.py:17
  83.6 0.8 iota_compare_fusion
  84.5 111.9 %all-reduce.3.cloned.1.call-done = f32[512,512]{0,1:T(8,128)} async-done(((f32[512,512]{0,1:T(8,128)}), f32[512,512]{0,1:T(8,128)}) %all-reduce.3.cloned.1.call-update) | async-done | bytes 1048592 | tf_op jit(solution)/shard_map/psum | solution.py:18
  196.4 1.6 copy.6
  198.0 1.4 fusion.9
  199.5 11.7 %cholesky.104 = f32[128,128]{1,0:T(8,128)S(1)} custom-call(f32[128,128]{1,0:T(8,128)S(1)} %cholesky.266), custom_call_target="Cholesky" | custom-call | tf_op jit(solution)/shard_map/jit(cholesky)/cholesky | solution.py:19
  211.2 9.8 %custom-call.30 = f32[1,128,128]{1,2,0:T(8,128)S(1)} custom-call(f32[1,128,128]{2,1,0:T(8,128)S(1)} %get-tuple-element.29), custom_call_target="InvertDiagBlocksLowerTriangular" | custom-call | tf_op jit(solution)/shard_map/jit(cholesky)/cholesky | solution.py:19
  221.8 11.7 %cholesky.217 = f32[128,128]{1,0:T(8,128)S(1)} custom-call(f32[128,128]{1,0:T(8,128)S(1)} %cholesky.270), custom_call_target="Cholesky" | custom-call | tf_op jit(solution)/shard_map/jit(cholesky)/cholesky | solution.py:19
  233.6 10.2 %custom-call.31 = f32[1,128,128]{1,2,0:T(8,128)S(1)} custom-call(f32[1,128,128]{2,1,0:T(8,128)S(1)} %get-tuple-element.26), custom_call_target="InvertDiagBlocksLowerTriangular" | custom-call | tf_op jit(solution)/shard_map/jit(cholesky)/cholesky | solution.py:19
  244.4 11.7 %cholesky.238 = f32[128,128]{1,0:T(8,128)S(1)} custom-call(f32[128,128]{1,0:T(8,128)S(1)} %cholesky.275), custom_call_target="Cholesky" | custom-call | tf_op jit(solution)/shard_map/jit(cholesky)/cholesky | solution.py:19
  256.8 9.8 %custom-call.32 = f32[1,128,128]{1,2,0:T(8,128)S(1)} custom-call(f32[1,128,128]{2,1,0:T(8,128)S(1)} %get-tuple-element.23), custom_call_target="InvertDiagBlocksLowerTriangular" | custom-call | tf_op jit(solution)/shard_map/jit(cholesky)/cholesky | solution.py:19
  267.3 11.7 %cholesky.255 = f32[128,128]{1,0:T(8,128)S(1)} custom-call(f32[128,128]{1,0:T(8,128)S(1)} %convolution_subtract_fusion.5), custom_call_target="Cholesky" | custom-call | tf_op jit(solution)/shard_map/jit(cholesky)/cholesky | solution.py:19
  279.7 0.9 compare_reduce_fusion.2
  283.3 10.3 %while.1 = (s32[]{:T(128)}, f32[512,512]{1,0:T(8,128)S(1)}, s32[4,2]{0,1:T(2,128)S(1)}, f32[4,128,128]{2,1,0:T(8,128)}, s32[]{:T(128)}) while((s32[]{:T(128)}, f32[512,512]{1,0:T(8,128)S(1)}, s32[4,2]{0,1:T(2,128)S(1)}, f32[4,128,128]{2,1,0:T(8,128)}, s32[]{:T(128)}) %tuple.31), condition=%wide.while_cond, body=%wide.while_body.sunk | while | flops 2 | bytes 132705 | solution.py:21
  283.9 2.0 bitcast_dynamic-update-slice_fusion.2
  286.4 2.0 bitcast_dynamic-update-slice_fusion.2
  289.0 2.0 bitcast_dynamic-update-slice_fusion.2
  291.6 2.0 bitcast_dynamic-update-slice_fusion.2
  293.6 40.1 %custom-call.33 = f32[4,128,128]{1,2,0:T(8,128)S(1)} custom-call(f32[4,128,128]{2,1,0:T(8,128)} %get-tuple-element.9), custom_call_target="InvertDiagBlocksLowerTriangular" | custom-call | tf_op jit(solution)/shard_map/triangular_solve | solution.py:21
  333.7 1.2 fusion.20
  337.7 14.6 %convolution_multiply_fusion = f32[2048,512]{1,0:T(8,128)S(1)} fusion(f32[512,2048]{1,0:T(8,128)S(1)} %copy-done.1, f32[128,512]{1,0:T(8,128)S(1)} %fusion.29, f32[128,512]{1,0:T(8,128)S(1)} %fusion.30, f32[128,512]{1,0:T(8,128)S(1)} %fusion.32, f32[128,512]{1,0:T(8,128)S(1)} %fusion.20), kind=kOutput, calls=%fused_computation.3 | convolution fusion | flops 6444285952 | bytes 9437184 | tf_op jit(solution)/shard_map/dot_general | solution.py:22
  352.3 1.9 copy-done.2
  354.2 6.1 %fusion = f32[512,2048]{1,0:T(8,128)} fusion(bf16[2048,2048]{1,0:T(8,128)(2,1)S(1)} %bitcast.58, f32[2048,512]{1,0:T(8,128)S(1)} %convolution_multiply_fusion), kind=kOutput, calls=%fused_computation.4 | convolution fusion | flops 4296015872 | bytes 16777216 | tf_op jit(solution)/shard_map/dot_general | solution.py:32
  361.0 3.1 dynamic-slice_select_fusion
  364.1 90.6 %reduce-scatter.2.cloned.1.call-done = f32[32,2048]{1,0:T(8,128)} async-done(((f32[512,2048]{1,0:T(8,128)}), f32[32,2048]{1,0:T(8,128)}) %reduce-scatter.2.cloned.1.call-update) | async-done | bytes 262160 | tf_op jit(solution)/shard_map/reduce_scatter | solution.py:31
  454.7 1.7 multiply_select_fusion
  (53 shorter events, 9.2 us)
Async XLA Ops:
  7.2 20.7 %all-gather.3.cloned.1.call-start = ((), (), s32[]{:S(2)}) async-start(), calls=%async_computation.1 | async-start | bytes 6291456 | tf_op jit(solution)/shard_map/all_gather | solution.py:14
  11.3 49.4 %all-gather.5.cloned.1.call-start = ((), (), s32[]{:S(2)}) async-start(), calls=%async_computation.2 | async-start | bytes 25165824 | tf_op jit(solution)/shard_map/all_gather | solution.py:13
  12.1 184.4 %all-reduce.3.cloned.1.call-start = ((), (), s32[]{:S(2)}) async-start(), calls=%async_computation.3 | async-start | bytes 2097152 | tf_op jit(solution)/shard_map/psum | solution.py:18
  73.7 1.9 copy-start
  83.4 371.3 %reduce-scatter.2.cloned.1.call-start = ((), (), s32[]{:S(2)}) async-start(), calls=%async_computation.4 | async-start | bytes 4456448 | tf_op jit(solution)/shard_map/reduce_scatter | solution.py:31
  333.7 4.0 copy-start.1
  336.6 17.6 %slice-start = ((s8[8388608]{0:T(1024)(128)(4,1)}), s8[4194304]{0:T(1024)(128)(4,1)S(1)}, s32[]{:S(2)}) async-start(s8[8388608]{0:T(1024)(128)(4,1)} %bitcast.57), calls=%async_computation.5 | async-start | bytes 8388608
  337.7 16.5 %slice-start.1 = ((s8[8388608]{0:T(1024)(128)(4,1)}), s8[4194304]{0:T(1024)(128)(4,1)S(1)}, s32[]{:S(2)}) async-start(s8[8388608]{0:T(1024)(128)(4,1)} %bitcast.57), calls=%async_computation.6 | async-start | bytes 8388608
  352.3 1.9 copy-start.2
Sparse Core Ops, SparseCore 0:
  11.4 16.3 all-gather.2
  29.4 31.2 all-gather.4
  83.5 112.8 all-reduce.2
  360.4 94.2 reduce-scatter.1
where the time goes:
time: 471 us; the launch traced here: 463 us
  waiting for transfers between devices  252 us (54%)
  other arithmetic  130 us (28%)
  matrix products  47.2 us (10%)
  between operations  17.5 us (4%)
  local copies, waits for them, and re-layouts  15.8 us (3%)
    psum x1, waiting for transfers between devices, on_device(): gram_matrix = lax.psum(local_gram, 'seq')  112 us
    reduce_scatter x1, waiting for transfers between devices, on_device(): lax.psum_scatter(lax.dot_general(rounded, key_rows, contract, preferred_e...  90.6 us
    another operation x14, other arithmetic, on_device(): lower_factor = jnp.linalg.cholesky(gram_matrix)  79 us
    another operation x3, other arithmetic, on_device(): lax.linalg.triangular_solve(lower_factor, identity, left_side=True, lower...  40.3 us
    all_gather x1, waiting for transfers between devices, on_device(): whole_keys = lax.all_gather(key_rows, 'grp', axis=1, tiled=True)  32.8 us
    all_gather x1, waiting for transfers between devices, on_device(): whole_probes = lax.all_gather(probes, 'grp', axis=0, tiled=True)  15.7 us
    dot_general x1, matrix products, on_device(): jnp.dot(sketch, inverse.T, precision=lax.Precision.HIGHEST) * root_tokens  14.6 us
    dot_general x1, matrix products, on_device(): jnp.dot(whole_keys, whole_probes, preferred_element_type=jnp.float32)  13 us
  transfers between devices with their start and end apart: 4, of which 4 were waited for; matrix products, arithmetic and copies ran while one was open for 1% of the time, Pallas kernels for 0%

commit v1 on v0

--- a/solution.py
+++ b/solution.py
@@ -3,6 +3,14 @@
 import jax.numpy as jnp
 from jax import lax
 from jax.sharding import PartitionSpec as P
+
+
+def sum_by_hops(array, axis):
+    size, acc = (lax.axis_size(axis), array)
+    for far in [1 << k for k in range(size.bit_length() - 1)]:
+        pairs = [(i, i ^ far) for i in range(size)]
+        acc = acc + lax.ppermute(acc, axis, pairs)
+    return acc
 
 
 def on_device(key_rows, probe_ints, rank_keep):
@@ -15,7 +23,7 @@
     sketch = jnp.dot(whole_keys, whole_probes, preferred_element_type=jnp.float32)
     contract = (((0,), (0,)), ((), ()))
     local_gram = lax.dot_general(sketch, sketch, contract, precision=lax.Precision.HIGHEST)
-    gram_matrix = lax.psum(local_gram, "seq")
+    gram_matrix = sum_by_hops(local_gram, "seq")
     lower_factor = jnp.linalg.cholesky(gram_matrix)
     identity = jnp.eye(gram_matrix.shape[0], dtype=jnp.float32)
     inverse = lax.linalg.triangular_solve(lower_factor, identity, left_side=True, lower=True)

time: 471 us -> 476 us (1.011)
  starting transfers between devices: 0.34 us -> 8.27 us
    psum x1 -> x0, waiting for transfers between devices: 112 us -> none  [on_device(): gram_matrix = lax.psum(local_gram, 'seq')]
    ppermute x0 -> x4, waiting for transfers between devices: none -> 112 us  [sum_by_hops(): acc = acc + lax.ppermute(acc, axis, pairs)]
    ppermute x0 -> x4, starting transfers between devices: none -> 8.15 us  [sum_by_hops(): acc = acc + lax.ppermute(acc, axis, pairs)]
  transfers between devices with their start and end apart: 4 -> 7, of which waited for: 4 -> 7; matrix products, arithmetic and copies ran while one was open for 1% -> 1% of each run, Pallas kernels for 0% -> 0%
where the time goes in v1:
time: 476 us; the launch traced here: 473 us
  waiting for transfers between devices  254 us (53%)
  other arithmetic  131 us (28%)
  matrix products  49.2 us (10%)
  between operations  17.4 us (4%)
  local copies, waits for them, and re-layouts  13.5 us (3%)
  starting transfers between devices  8.27 us (2%)
    ppermute x4, waiting for transfers between devices, sum_by_hops(): acc = acc + lax.ppermute(acc, axis, pairs)  112 us
    reduce_scatter x1, waiting for transfers between devices, on_device(): lax.psum_scatter(lax.dot_general(rounded, key_rows, contract, preferred_e...  92.7 us
    another operation x14, other arithmetic, on_device(): lower_factor = jnp.linalg.cholesky(gram_matrix)  79 us
    another operation x3, other arithmetic, on_device(): lax.linalg.triangular_solve(lower_factor, identity, left_side=True, lower...  40.4 us
    all_gather x1, waiting for transfers between devices, on_device(): whole_keys = lax.all_gather(key_rows, 'grp', axis=1, tiled=True)  32.8 us
    all_gather x1, waiting for transfers between devices, on_device(): whole_probes = lax.all_gather(probes, 'grp', axis=0, tiled=True)  15.7 us
    dot_general x1, matrix products, on_device(): jnp.dot(sketch, inverse.T, precision=lax.Precision.HIGHEST) * root_tokens  14.6 us
    dot_general x1, matrix products, on_device(): jnp.dot(whole_keys, whole_probes, preferred_element_type=jnp.float32)  13.2 us
  transfers between devices with their start and end apart: 7, of which 7 were waited for; matrix products, arithmetic and copies ran while one was open for 1% of the time, Pallas kernels for 0%

profile of v1, /device:TPU:0, one launch (start us, length us, event | category | flops | bytes accessed | tf_op | source)
XLA Modules:
  0.0 472.8 jit_solution(11982758630215182708)
XLA Ops:
  7.2 4.1 multiply_convert_fusion
  12.1 15.7 %all-gather.3.cloned.1.call-done = bf16[4096,512]{1,0:T(8,128)(2,1)} async-done(((bf16[2048,512]{1,0:T(8,128)(2,1)}), bf16[4096,512]{1,0:T(8,128)(2,1)}) %all-gather.3.cloned.1.call-update) | async-done | bytes 4194320 | tf_op jit(solution)/shard_map/all_gather | solution.py:22
  27.8 32.8 %all-gather.5.cloned.1.call-done = bf16[2048,4096]{1,0:T(8,128)(2,1)} async-done(((bf16[2048,2048]{1,0:T(8,128)(2,1)}), bf16[2048,4096]{1,0:T(8,128)(2,1)}) %all-gather.5.cloned.1.call-update) | async-done | bytes 16777232 | tf_op jit(solution)/shard_map/all_gather | solution.py:21
  60.7 13.2 %fusion.47 = f32[512,2048]{1,0:T(8,128)S(1)} fusion(bf16[4096,512]{1,0:T(8,128)(2,1)} %all-gather.3.cloned.1.call-done, bf16[2048,4096]{1,0:T(8,128)(2,1)} %all-gather.5.cloned.1.call-done), kind=kOutput, calls=%fused_computation.87 | convolution fusion | flops 8589934592 | bytes 25165824 | tf_op jit(solution)/shard_map/dot_general | solution.py:23
  73.9 6.7 %fusion.48 = f32[512,512]{0,1:T(8,128)S(1)} fusion(f32[512,2048]{1,0:T(8,128)S(1)} %fusion.47), kind=kOutput, calls=%fused_computation.88 | convolution fusion | flops 6442450944 | bytes 5242880 | tf_op jit(solution)/shard_map/dot_general | solution.py:25
  80.7 1.8 collective-permute-start
  82.5 23.6 %collective-permute-done = f32[512,512]{0,1:T(8,128)S(1)} collective-permute-done((f32[512,512]{0,1:T(8,128)S(1)}, f32[512,512]{0,1:T(8,128)S(1)}, u32[]{:S(2)}, u32[]{:S(2)}) %collective-permute-start) | collective-permute-done | bytes 1048608 | tf_op jit(solution)/shard_map/ppermute | solution.py:12
  106.3 1.8 collective-permute-start.1
  108.1 22.8 %collective-permute-done.1 = f32[512,512]{0,1:T(8,128)S(1)} collective-permute-done((f32[512,512]{0,1:T(8,128)S(1)}, f32[512,512]{0,1:T(8,128)S(1)}, u32[]{:S(2)}, u32[]{:S(2)}) %collective-permute-start.1) | collective-permute-done | bytes 1048608 | tf_op jit(solution)/shard_map/ppermute | solution.py:12
  131.1 1.8 collective-permute-start.2
  133.0 21.9 %collective-permute-done.2 = f32[512,512]{0,1:T(8,128)S(1)} collective-permute-done((f32[512,512]{0,1:T(8,128)S(1)}, f32[512,512]{0,1:T(8,128)S(1)}, u32[]{:S(2)}, u32[]{:S(2)}) %collective-permute-start.2) | collective-permute-done | bytes 1048608 | tf_op jit(solution)/shard_map/ppermute | solution.py:12
  155.1 2.7 collective-permute-start.3
  158.0 43.3 %collective-permute-done.3 = f32[512,512]{0,1:T(8,128)} collective-permute-done((f32[512,512]{0,1:T(8,128)S(1)}, f32[512,512]{0,1:T(8,128)}, u32[]{:S(2)}, u32[]{:S(2)}) %collective-permute-start.3) | collective-permute-done | bytes 1048608 | tf_op jit(solution)/shard_map/ppermute | solution.py:12
  204.3 11.9 %cholesky.104 = f32[128,128]{1,0:T(8,128)S(1)} custom-call(f32[128,128]{1,0:T(8,128)S(1)} %cholesky.266), custom_call_target="Cholesky" | custom-call | tf_op jit(solution)/shard_map/jit(cholesky)/cholesky | solution.py:27
  216.3 9.8 %custom-call.30 = f32[1,128,128]{1,2,0:T(8,128)S(1)} custom-call(f32[1,128,128]{2,1,0:T(8,128)S(1)} %get-tuple-element.29), custom_call_target="InvertDiagBlocksLowerTriangular" | custom-call | tf_op jit(solution)/shard_map/jit(cholesky)/cholesky | solution.py:27
  228.7 11.7 %cholesky.217 = f32[128,128]{1,0:T(8,128)S(1)} custom-call(f32[128,128]{1,0:T(8,128)S(1)} %cholesky.270), custom_call_target="Cholesky" | custom-call | tf_op jit(solution)/shard_map/jit(cholesky)/cholesky | solution.py:27
  240.5 9.8 %custom-call.31 = f32[1,128,128]{1,2,0:T(8,128)S(1)} custom-call(f32[1,128,128]{2,1,0:T(8,128)S(1)} %get-tuple-element.26), custom_call_target="InvertDiagBlocksLowerTriangular" | custom-call | tf_op jit(solution)/shard_map/jit(cholesky)/cholesky | solution.py:27
  251.9 12.1 %cholesky.238 = f32[128,128]{1,0:T(8,128)S(1)} custom-call(f32[128,128]{1,0:T(8,128)S(1)} %cholesky.275), custom_call_target="Cholesky" | custom-call | tf_op jit(solution)/shard_map/jit(cholesky)/cholesky | solution.py:27
  264.7 9.8 %custom-call.32 = f32[1,128,128]{1,2,0:T(8,128)S(1)} custom-call(f32[1,128,128]{2,1,0:T(8,128)S(1)} %get-tuple-element.23), custom_call_target="InvertDiagBlocksLowerTriangular" | custom-call | tf_op jit(solution)/shard_map/jit(cholesky)/cholesky | solution.py:27
  275.9 11.7 %cholesky.255 = f32[128,128]{1,0:T(8,128)S(1)} custom-call(f32[128,128]{1,0:T(8,128)S(1)} %slice_subtract_fusion.2), custom_call_target="Cholesky" | custom-call | tf_op jit(solution)/shard_map/jit(cholesky)/cholesky | solution.py:27
  291.6 10.1 %while.1 = (s32[]{:T(128)}, f32[512,512]{1,0:T(8,128)S(1)}, s32[4,2]{0,1:T(2,128)S(1)}, f32[4,128,128]{2,1,0:T(8,128)}, s32[]{:T(128)}) while((s32[]{:T(128)}, f32[512,512]{1,0:T(8,128)S(1)}, s32[4,2]{0,1:T(2,128)S(1)}, f32[4,128,128]{2,1,0:T(8,128)}, s32[]{:T(128)}) %tuple.31), condition=%wide.while_cond, body=%wide.while_body.sunk | while | flops 2 | bytes 132705 | solution.py:29
  292.2 1.9 bitcast_dynamic-update-slice_fusion.2
  294.7 1.9 bitcast_dynamic-update-slice_fusion.2
  297.3 1.9 bitcast_dynamic-update-slice_fusion.2
  299.8 1.9 bitcast_dynamic-update-slice_fusion.2
  301.7 40.3 %custom-call.33 = f32[4,128,128]{1,2,0:T(8,128)S(1)} custom-call(f32[4,128,128]{2,1,0:T(8,128)} %get-tuple-element.9), custom_call_target="InvertDiagBlocksLowerTriangular" | custom-call | tf_op jit(solution)/shard_map/triangular_solve | solution.py:29
  345.1 14.6 %convolution_multiply_fusion = f32[2048,512]{1,0:T(8,128)S(1)} fusion(f32[512,2048]{1,0:T(8,128)S(1)} %copy-done.1, f32[128,512]{1,0:T(8,128)S(1)} %fusion.31, f32[128,512]{1,0:T(8,128)S(1)} %fusion.32, f32[128,512]{1,0:T(8,128)S(1)} %fusion.34, f32[128,512]{1,0:T(8,128)S(1)} %fusion.21), kind=kOutput, calls=%fused_computation.3 | convolution fusion | flops 6444285952 | bytes 9437184 | tf_op jit(solution)/shard_map/dot_general | solution.py:30
  359.7 1.9 copy-done.2
  361.7 6.2 %fusion = f32[512,2048]{1,0:T(8,128)} fusion(bf16[2048,2048]{1,0:T(8,128)(2,1)S(1)} %bitcast.58, f32[2048,512]{1,0:T(8,128)S(1)} %convolution_multiply_fusion), kind=kOutput, calls=%fused_computation.4 | convolution fusion | flops 4296015872 | bytes 16777216 | tf_op jit(solution)/shard_map/dot_general | solution.py:40
  368.6 3.1 dynamic-slice_select_fusion
  371.7 92.7 %reduce-scatter.2.cloned.1.call-done = f32[32,2048]{1,0:T(8,128)} async-done(((f32[512,2048]{1,0:T(8,128)}), f32[32,2048]{1,0:T(8,128)}) %reduce-scatter.2.cloned.1.call-update) | async-done | bytes 262160 | tf_op jit(solution)/shard_map/reduce_scatter | solution.py:39
  464.3 1.7 multiply_select_fusion
  (64 shorter events, 17.9 us)
Async XLA Ops:
  7.2 20.7 %all-gather.3.cloned.1.call-start = ((), (), s32[]{:S(2)}) async-start(), calls=%async_computation.1 | async-start | bytes 6291456 | tf_op jit(solution)/shard_map/all_gather | solution.py:22
  11.3 49.4 %all-gather.5.cloned.1.call-start = ((), (), s32[]{:S(2)}) async-start(), calls=%async_computation.2 | async-start | bytes 25165824 | tf_op jit(solution)/shard_map/all_gather | solution.py:21
  12.1 452.3 %reduce-scatter.2.cloned.1.call-start = ((), (), s32[]{:S(2)}) async-start(), calls=%async_computation.3 | async-start | bytes 4456448 | tf_op jit(solution)/shard_map/reduce_scatter | solution.py:39
  73.9 6.8 %copy-start = (f32[512,2048]{1,0:T(8,128)}, f32[512,2048]{1,0:T(8,128)S(1)}, u32[]{:S(2)}) copy-start(f32[512,2048]{1,0:T(8,128)S(1)} %fusion.47) | copy-start | bytes 12582916
  80.7 25.4 %collective-permute-start = (f32[512,512]{0,1:T(8,128)S(1)}, f32[512,512]{0,1:T(8,128)S(1)}, u32[]{:S(2)}, u32[]{:S(2)}) collective-permute-start(f32[512,512]{0,1:T(8,128)S(1)} %fusion.48), channel_id=1, source_target_pairs={{0,2},{2,0},{4,6},{6,4},{8,10},{10,8},{12,14},{14,12},{16,18},{18,... | collective-permute-start | bytes 3145736 | tf_op jit(solution)/shard_map/ppermute | solution.py:12
  106.3 24.6 %collective-permute-start.1 = (f32[512,512]{0,1:T(8,128)S(1)}, f32[512,512]{0,1:T(8,128)S(1)}, u32[]{:S(2)}, u32[]{:S(2)}) collective-permute-start(f32[512,512]{0,1:T(8,128)S(1)} %add.79), channel_id=1, source_target_pairs={{0,4},{2,6},{4,0},{6,2},{8,12},{10,14},{12,8},{14,10},{16,20},{18,... | collective-permute-start | bytes 3145736 | tf_op jit(solution)/shard_map/ppermute | solution.py:12
  131.1 23.7 %collective-permute-start.2 = (f32[512,512]{0,1:T(8,128)S(1)}, f32[512,512]{0,1:T(8,128)S(1)}, u32[]{:S(2)}, u32[]{:S(2)}) collective-permute-start(f32[512,512]{0,1:T(8,128)S(1)} %add.80), channel_id=1, source_target_pairs={{0,8},{2,10},{4,12},{6,14},{8,0},{10,2},{12,4},{14,6},{16,24},{18,... | collective-permute-start | bytes 3145736 | tf_op jit(solution)/shard_map/ppermute | solution.py:12
  155.1 46.3 %collective-permute-start.3 = (f32[512,512]{0,1:T(8,128)S(1)}, f32[512,512]{0,1:T(8,128)}, u32[]{:S(2)}, u32[]{:S(2)}) collective-permute-start(f32[512,512]{0,1:T(8,128)S(1)} %add.81), channel_id=1, source_target_pairs={{0,16},{2,18},{4,20},{6,22},{8,24},{10,26},{12,28},{14,30},{16,0},... | collective-permute-start | bytes 3145736 | tf_op jit(solution)/shard_map/ppermute | solution.py:12
  203.3 1.0 copy-start.3
  342.0 3.1 copy-start.1
  344.0 17.6 %slice-start = ((s8[8388608]{0:T(1024)(128)(4,1)}), s8[4194304]{0:T(1024)(128)(4,1)S(1)}, s32[]{:S(2)}) async-start(s8[8388608]{0:T(1024)(128)(4,1)} %bitcast.57), calls=%async_computation.4 | async-start | bytes 8388608
  345.1 16.5 %slice-start.1 = ((s8[8388608]{0:T(1024)(128)(4,1)}), s8[4194304]{0:T(1024)(128)(4,1)S(1)}, s32[]{:S(2)}) async-start(s8[8388608]{0:T(1024)(128)(4,1)} %bitcast.57), calls=%async_computation.5 | async-start | bytes 8388608
  359.7 1.9 copy-start.2
Sparse Core Ops, SparseCore 0:
  11.4 16.3 all-gather.2
  29.4 31.2 all-gather.4
  368.0 96.2 reduce-scatter.1
